TPU v7x, 1024 devices: a whole 4x4x32 slice. The times are simulated.
1024 devices in a mesh: node: 64 (over z, core), local: 4 (over y), tp: 4 (over x).
Axes of the slice: x: 4, y: 4, z: 32, core: 2. Of those that a mesh axis runs over, the one named last changes fastest.
Arguments:
- tokens: bfloat16 [8192, 2048], P(('node', 'local'), 'tp'), may hold values from -6 to 6
- grad_out: bfloat16 [8192, 2048], P(('node', 'local'), 'tp'), may hold values from -6 to 6
- routes: int32 [8192, 8], P(('node', 'local')), may hold values from 0 to 127, all different within a row; in each aligned block of 32 rows (0 to 31, 32 to 63, ...) at most 3 rows name the same one
- route_weight: float32 [8192, 8], P(('node', 'local')), may hold values from 0.05 to 0.5
- w_gate: bfloat16 [256, 2048, 384], P(('node', 'local'), 'tp'), may hold values from -0.125 to 0.125
- w_up: bfloat16 [256, 2048, 384], P(('node', 'local'), 'tp'), may hold values from -0.125 to 0.125
- w_down: bfloat16 [256, 384, 2048], P(('node', 'local'), None, 'tp'), may hold values from -0.21875 to 0.21875
Outputs:
- mixed: bfloat16 [8192, 2048], P(('node', 'local'), 'tp')
- grad_tokens: bfloat16 [8192, 2048], P(('node', 'local'), 'tp')
- grad_gate: bfloat16 [256, 2048, 384], P(('node', 'local'), 'tp')
- grad_up: bfloat16 [256, 2048, 384], P(('node', 'local'), 'tp')
- grad_down: bfloat16 [256, 384, 2048], P(('node', 'local'), None, 'tp')
Inputs may be any that keep to these rules, and one draw needn't show every extreme that they name: `routes`: each row names 8 different experts; within each aligned block of 32 rows (the tokens of one index of node and local) no expert is named more than 3 times, a bound that some block reaches.
All inputs are finite; a program needn't handle non-finite values.
Results may differ from a plain program's by a relative error of at most 0.02.
Values may be sent and summed in bfloat16 or wider, within the bound.
A program may use at most 32 MiB of HBM per device.

v0:
```python
import jax
import jax.numpy as jnp
from jax import lax
from jax.sharding import PartitionSpec as P


def slot_table(route_rows, experts, capacity):
    flat = route_rows.reshape(-1)
    count = flat.shape[0]
    onehot = (flat[:, None] == jnp.arange(experts, dtype=jnp.int32)[None, :]).astype(jnp.float32)
    lower = (jnp.arange(count)[:, None] > jnp.arange(count)[None, :]).astype(jnp.float32)
    before = jnp.dot(lower, onehot, precision=lax.Precision.HIGHEST)
    ranking = jnp.sum(before * onehot, axis=1).astype(jnp.int32)
    position = flat * capacity + ranking
    return (position[None, :] == jnp.arange(experts * capacity, dtype=jnp.int32)[:, None]).astype(
        jnp.float32
    )


def activate(gate, up_val, d_hidden):
    sig_gate = jax.nn.sigmoid(gate)
    activated = gate * sig_gate
    hidden = (activated * up_val).astype(jnp.bfloat16)
    d_gate = (d_hidden * up_val * sig_gate * (1.0 + gate * (1.0 - sig_gate))).astype(jnp.bfloat16)
    d_up = (d_hidden * activated).astype(jnp.bfloat16)
    return (hidden, d_gate, d_up)


def shards(tokens, grad_out, routes, route_weight, w_gate, w_up, w_down):
    n_node = lax.axis_size("node")
    n_local = lax.axis_size("local")
    experts = n_node * n_local // 2
    exp_node = n_local // 2
    tok_rows, features = tokens.shape
    topk = routes.shape[1]
    capacity = min(tok_rows, max(2, 3 * tok_rows * topk // (2 * experts)))
    table = slot_table(routes, experts, capacity)
    token_map = table.reshape(experts * capacity, tok_rows, topk).sum(-1).astype(jnp.bfloat16)
    table_low = table.astype(jnp.bfloat16)
    send_rows = jnp.dot(token_map, tokens, preferred_element_type=jnp.float32).astype(jnp.bfloat16)
    weights_flat = route_weight.reshape(-1)
    scaled = (
        weights_flat[:, None] * jnp.repeat(grad_out, topk, axis=0).astype(jnp.float32)
    ).astype(jnp.bfloat16)
    send_grads = jnp.dot(table_low, scaled, preferred_element_type=jnp.float32).astype(jnp.bfloat16)
    send_rows = send_rows.reshape(n_node, exp_node, capacity, features)
    send_grads = send_grads.reshape(n_node, exp_node, capacity, features)
    twice_rows = jnp.repeat(send_rows, 2, axis=1)
    twice_grads = jnp.repeat(send_grads, 2, axis=1)
    got_rows, got_grads = (
        lax.all_to_all(
            lax.all_to_all(twice_rows, "node", split_axis=0, concat_axis=2, tiled=True),
            "local",
            split_axis=1,
            concat_axis=2,
            tiled=True,
        ),
        lax.all_to_all(
            lax.all_to_all(twice_grads, "node", split_axis=0, concat_axis=2, tiled=True),
            "local",
            split_axis=1,
            concat_axis=2,
            tiled=True,
        ),
    )
    rows_all = got_rows.shape[2]
    got_rows = got_rows.reshape(rows_all, features)
    got_grads = got_grads.reshape(rows_all, features)
    weight_g = w_gate[0]
    weight_u = w_up[0]
    weight_d = w_down[0]
    contract_last = (((1,), (1,)), ((), ()))
    contract_first = (((0,), (0,)), ((), ()))
    gate_part = jnp.dot(got_rows, weight_g, preferred_element_type=jnp.float32)
    up_part = jnp.dot(got_rows, weight_u, preferred_element_type=jnp.float32)
    hidden_part = lax.dot_general(
        got_grads, weight_d, contract_last, preferred_element_type=jnp.float32
    )
    gate, up_val, d_hidden = (
        lax.psum(gate_part.astype(jnp.bfloat16), "tp").astype(jnp.float32),
        lax.psum(up_part.astype(jnp.bfloat16), "tp").astype(jnp.float32),
        lax.psum(hidden_part.astype(jnp.bfloat16), "tp").astype(jnp.float32),
    )
    hidden, d_gate, d_up = activate(gate, up_val, d_hidden)
    grad_wd = lax.dot_general(
        hidden, got_grads, contract_first, preferred_element_type=jnp.float32
    ).astype(jnp.bfloat16)
    grad_wg = lax.dot_general(
        got_rows, d_gate, contract_first, preferred_element_type=jnp.float32
    ).astype(jnp.bfloat16)
    grad_wu = lax.dot_general(
        got_rows, d_up, contract_first, preferred_element_type=jnp.float32
    ).astype(jnp.bfloat16)
    out_sum = jnp.dot(hidden, weight_d, preferred_element_type=jnp.float32).astype(jnp.bfloat16)
    back_sum = (
        lax.dot_general(d_gate, weight_g, contract_last, preferred_element_type=jnp.float32)
        + lax.dot_general(d_up, weight_u, contract_last, preferred_element_type=jnp.float32)
    ).astype(jnp.bfloat16)
    out_sum = out_sum.reshape(1, n_local, n_node * capacity, features)
    back_sum = back_sum.reshape(1, n_local, n_node * capacity, features)
    ret_out, ret_back = (
        lax.all_to_all(
            lax.all_to_all(out_sum, "node", split_axis=2, concat_axis=0, tiled=True),
            "local",
            split_axis=1,
            concat_axis=1,
            tiled=True,
        ),
        lax.all_to_all(
            lax.all_to_all(back_sum, "node", split_axis=2, concat_axis=0, tiled=True),
            "local",
            split_axis=1,
            concat_axis=1,
            tiled=True,
        ),
    )
    slot_out = ret_out.astype(jnp.float32).reshape(n_node, exp_node, 2, capacity, features).sum(2)
    slot_back = ret_back.astype(jnp.float32).reshape(n_node, exp_node, 2, capacity, features).sum(2)
    slot_out = slot_out.astype(jnp.bfloat16)
    slot_back = slot_back.astype(jnp.bfloat16)
    slot_out = slot_out.reshape(experts * capacity, features)
    slot_back = slot_back.reshape(experts * capacity, features)
    gathered = lax.dot_general(
        table_low, slot_out, contract_first, preferred_element_type=jnp.float32
    )
    mixed = jnp.sum(
        gathered.reshape(tok_rows, topk, features) * route_weight[..., None], axis=1
    ).astype(jnp.bfloat16)
    grad_tokens = lax.dot_general(
        token_map, slot_back, contract_first, preferred_element_type=jnp.float32
    ).astype(jnp.bfloat16)
    return (mixed, grad_tokens, grad_wg[None], grad_wu[None], grad_wd[None])


def solution(mesh):
    return jax.shard_map(
        shards,
        mesh=mesh,
        in_specs=(
            P(("node", "local"), "tp"),
            P(("node", "local"), "tp"),
            P(("node", "local"), None),
            P(("node", "local"), None),
            P(("node", "local"), "tp", None),
            P(("node", "local"), "tp", None),
            P(("node", "local"), None, "tp"),
        ),
        out_specs=(
            P(("node", "local"), "tp"),
            P(("node", "local"), "tp"),
            P(("node", "local"), "tp", None),
            P(("node", "local"), "tp", None),
            P(("node", "local"), None, "tp"),
        ),
        check_vma=False,
    )
```

profile of v0, /device:TPU:32, one launch (start us, length us, event | category | flops | bytes accessed | tf_op | source)
XLA Modules:
  0.0 570.0 jit_solution(12828668889805167665)
XLA Ops:
  12.6 29.1 %all-to-all-start = ((bf16[64,4,3,512]{3,1,2,0:T(4,128)(2,1)}), bf16[64,4,3,512]{3,1,2,0:T(4,128)(2,1)S(1)}, u32[]{:S(2)}, u32[]{:S(2)}) async-start(bf16[64,4,3,512]{3,1,2,0:T(4,128)(2,1)} %reshape.119), calls=%async_computation | async-start | bytes 1572864 | tf_op jit(solution)/shard_map/all_to_all | solution.py:52
  45.2 83.8 %all-to-all-done = bf16[64,4,3,512]{3,1,2,0:T(4,128)(2,1)S(1)} async-done(((bf16[64,4,3,512]{3,1,2,0:T(4,128)(2,1)}), bf16[64,4,3,512]{3,1,2,0:T(4,128)(2,1)S(1)}, u32[]{:S(2)}, u32[]{:S(2)}) %all-to-all-start) | async-done | bytes 786464 | tf_op jit(solution)/shard_map/all_to_all | solution.py:52
  129.0 5.5 all-to-all-start.4
  135.6 86.3 %all-to-all-done.4 = bf16[64,4,3,512]{3,1,2,0:T(4,128)(2,1)S(1)} async-done(((bf16[64,4,3,512]{3,1,2,0:T(4,128)(2,1)}), bf16[64,4,3,512]{3,1,2,0:T(4,128)(2,1)S(1)}, u32[]{:S(2)}, u32[]{:S(2)}) %all-to-all-start.4) | async-done | bytes 786464 | tf_op jit(solution)/shard_map/all_to_all | solution.py:59
  221.8 4.5 all-to-all-start.1
  227.3 10.4 %all-to-all-done.1 = bf16[1,4,192,512]{3,2,0,1:T(8,128)(2,1)S(1)} async-done(((bf16[1,4,192,512]{3,2,0,1:T(8,128)(2,1)}), bf16[1,4,192,512]{3,2,0,1:T(8,128)(2,1)S(1)}, u32[]{:S(2)}, u32[]{:S(2)}) %all-to-all-start.1) | async-done | bytes 786464 | tf_op jit(solution)/shard_map/all_to_all | solution.py:51
  237.8 3.5 all-to-all-start.5
  244.1 7.4 %all-to-all-done.5 = bf16[1,4,192,512]{3,2,0,1:T(8,128)(2,1)S(1)} async-done(((bf16[1,4,192,512]{3,2,0,1:T(8,128)(2,1)}), bf16[1,4,192,512]{3,2,0,1:T(8,128)(2,1)S(1)}, u32[]{:S(2)}, u32[]{:S(2)}) %all-to-all-start.5) | async-done | bytes 786464 | tf_op jit(solution)/shard_map/all_to_all | solution.py:58
  253.0 72.0 %all-reduce.3.cloned.1.call-done = (bf16[768,384]{1,0:T(8,128)(2,1)}, bf16[768,384]{1,0:T(8,128)(2,1)}, bf16[768,384]{1,0:T(8,128)(2,1)}) async-done(((bf16[768,384]{1,0:T(8,128)(2,1)}, bf16[768,384]{1,0:T(8,128)(2,1)}, bf16[768,384]{1,0:T(8,128)(2,1)}), (bf16[768,384]{1,0:T(8,128)(2,1)}, bf16[768,384]{1,0:T(8,128)(2,1)}, bf16[768,384]{1,0:T(8,128)(2,1)})) %all-reduce.3.cloned.1.call-update) | async-done | bytes 1769488 | tf_op jit(solution)/shard_map/psum | solution.py:81
  325.0 1.9 convolution_convert_fusion
  326.8 1.5 copy.69
  328.3 23.6 %all-to-all-start.2 = ((bf16[1,4,192,512]{3,1,0,2:T(4,128)(2,1)}), bf16[1,4,192,512]{3,1,0,2:T(4,128)(2,1)S(1)}, u32[]{:S(2)}, u32[]{:S(2)}) async-start(bf16[1,4,192,512]{3,1,0,2:T(4,128)(2,1)} %copy.69), calls=%async_computation.2 | async-start | bytes 1572864 | tf_op jit(solution)/shard_map/all_to_all | solution.py:103
  351.9 2.0 fusion.6
  356.6 1.5 copy.77
  358.1 81.0 %all-to-all-done.2 = bf16[1,4,192,512]{3,1,0,2:T(4,128)(2,1)S(1)} async-done(((bf16[1,4,192,512]{3,1,0,2:T(4,128)(2,1)}), bf16[1,4,192,512]{3,1,0,2:T(4,128)(2,1)S(1)}, u32[]{:S(2)}, u32[]{:S(2)}) %all-to-all-start.2) | async-done | bytes 786464 | tf_op jit(solution)/shard_map/all_to_all | solution.py:103
  439.1 5.5 all-to-all-start.6
  445.7 86.3 %all-to-all-done.6 = bf16[1,4,192,512]{3,1,0,2:T(4,128)(2,1)S(1)} async-done(((bf16[1,4,192,512]{3,1,0,2:T(4,128)(2,1)}), bf16[1,4,192,512]{3,1,0,2:T(4,128)(2,1)S(1)}, u32[]{:S(2)}, u32[]{:S(2)}) %all-to-all-start.6) | async-done | bytes 786464 | tf_op jit(solution)/shard_map/all_to_all | solution.py:110
  532.0 4.3 all-to-all-start.3
  536.2 2.5 fusion
  538.8 1.4 fusion.1
  541.3 6.4 %all-to-all-done.3 = bf16[64,4,3,512]{3,0,2,1:T(8,128)(2,1)S(1)} async-done(((bf16[64,4,3,512]{3,0,2,1:T(8,128)(2,1)}), bf16[64,4,3,512]{3,0,2,1:T(8,128)(2,1)S(1)}, u32[]{:S(2)}, u32[]{:S(2)}) %all-to-all-start.3) | async-done | bytes 786464 | tf_op jit(solution)/shard_map/all_to_all | solution.py:102
  547.7 3.5 all-to-all-start.7
  551.2 2.4 fusion.2
  555.5 6.0 %all-to-all-done.7 = bf16[64,4,3,512]{3,0,2,1:T(8,128)(2,1)S(1)} async-done(((bf16[64,4,3,512]{3,0,2,1:T(8,128)(2,1)}), bf16[64,4,3,512]{3,0,2,1:T(8,128)(2,1)S(1)}, u32[]{:S(2)}, u32[]{:S(2)}) %all-to-all-start.7) | async-done | bytes 786464 | tf_op jit(solution)/shard_map/all_to_all | solution.py:109
  (70 shorter events, 23.4 us)
Async XLA Ops:
  7.2 244.4 %copy-start = (bf16[1,384,512]{2,1,0:T(8,128)(2,1)S(1)}, bf16[1,384,512]{2,1,0:T(8,128)(2,1)}, u32[]{:S(2)}) copy-start(bf16[1,384,512]{2,1,0:T(8,128)(2,1)} %param.13) | copy-start | bytes 1179652
  8.6 0.6 copy-start.9
  11.4 30.4 %copy-start.14 = (f32[32,8]{0,1:T(8,128)S(1)}, f32[32,8]{0,1:T(8,128)}, u32[]{:S(2)}) copy-start(f32[32,8]{0,1:T(8,128)} %param.10) | copy-start | bytes 3076
  12.6 29.9 %copy-start.13 = (bf16[32,512]{1,0:T(8,128)(2,1)S(1)}, bf16[32,512]{1,0:T(8,128)(2,1)}, u32[]{:S(2)}) copy-start(bf16[32,512]{1,0:T(8,128)(2,1)} %param.8) | copy-start | bytes 98308
  12.6 116.4 %all-to-all-start = ((bf16[64,4,3,512]{3,1,2,0:T(4,128)(2,1)}), bf16[64,4,3,512]{3,1,2,0:T(4,128)(2,1)S(1)}, u32[]{:S(2)}, u32[]{:S(2)}) async-start(bf16[64,4,3,512]{3,1,2,0:T(4,128)(2,1)} %reshape.119), calls=%async_computation | async-start | bytes 1572864 | tf_op jit(solution)/shard_map/all_to_all | solution.py:52
  41.8 0.6 copy-start.11
  129.0 92.8 %all-to-all-start.4 = ((bf16[64,4,3,512]{3,1,2,0:T(4,128)(2,1)}), bf16[64,4,3,512]{3,1,2,0:T(4,128)(2,1)S(1)}, u32[]{:S(2)}, u32[]{:S(2)}) async-start(bf16[64,4,3,512]{3,1,2,0:T(4,128)(2,1)} %reshape.125), calls=%async_computation.4 | async-start | bytes 1572864 | tf_op jit(solution)/shard_map/all_to_all | solution.py:59
  221.8 15.9 %all-to-all-start.1 = ((bf16[1,4,192,512]{3,2,0,1:T(8,128)(2,1)}), bf16[1,4,192,512]{3,2,0,1:T(8,128)(2,1)S(1)}, u32[]{:S(2)}, u32[]{:S(2)}) async-start(bf16[1,4,192,512]{3,2,0,1:T(8,128)(2,1)} %copy.68), calls=%async_computation.1 | async-start | bytes 1572864 | tf_op jit(solution)/shard_map/all_to_all | solution.py:51
  227.3 14.0 %copy-start.8 = (bf16[1,512,384]{2,1,0:T(8,128)(2,1)S(1)}, bf16[1,512,384]{2,1,0:T(8,128)(2,1)}, u32[]{:S(2)}) copy-start(bf16[1,512,384]{2,1,0:T(8,128)(2,1)} %param.12) | copy-start | bytes 1179652
  237.8 13.8 %all-to-all-start.5 = ((bf16[1,4,192,512]{3,2,0,1:T(8,128)(2,1)}), bf16[1,4,192,512]{3,2,0,1:T(8,128)(2,1)S(1)}, u32[]{:S(2)}, u32[]{:S(2)}) async-start(bf16[1,4,192,512]{3,2,0,1:T(8,128)(2,1)} %copy.76), calls=%async_computation.5 | async-start | bytes 1572864 | tf_op jit(solution)/shard_map/all_to_all | solution.py:58
  241.3 1.5 copy-start.2
  241.3 83.7 %all-reduce.3.cloned.1.call-start = ((), (), s32[]{:S(2)}) async-start(), calls=%async_computation.8 | async-start | bytes 3538944 | tf_op jit(solution)/shard_map/psum | solution.py:81
  328.3 110.8 %all-to-all-start.2 = ((bf16[1,4,192,512]{3,1,0,2:T(4,128)(2,1)}), bf16[1,4,192,512]{3,1,0,2:T(4,128)(2,1)S(1)}, u32[]{:S(2)}, u32[]{:S(2)}) async-start(bf16[1,4,192,512]{3,1,0,2:T(4,128)(2,1)} %copy.69), calls=%async_computation.2 | async-start | bytes 1572864 | tf_op jit(solution)/shard_map/all_to_all | solution.py:103
  353.9 0.8 copy-start.1
  354.7 1.1 copy-start.4
  354.7 1.2 copy-start.6
  439.1 92.8 %all-to-all-start.6 = ((bf16[1,4,192,512]{3,1,0,2:T(4,128)(2,1)}), bf16[1,4,192,512]{3,1,0,2:T(4,128)(2,1)S(1)}, u32[]{:S(2)}, u32[]{:S(2)}) async-start(bf16[1,4,192,512]{3,1,0,2:T(4,128)(2,1)} %copy.77), calls=%async_computation.6 | async-start | bytes 1572864 | tf_op jit(solution)/shard_map/all_to_all | solution.py:110
  532.0 15.7 %all-to-all-start.3 = ((bf16[64,4,3,512]{3,0,2,1:T(8,128)(2,1)}), bf16[64,4,3,512]{3,0,2,1:T(8,128)(2,1)S(1)}, u32[]{:S(2)}, u32[]{:S(2)}) async-start(bf16[64,4,3,512]{3,0,2,1:T(8,128)(2,1)} %copy.70), calls=%async_computation.3 | async-start | bytes 1572864 | tf_op jit(solution)/shard_map/all_to_all | solution.py:102
  536.2 2.5 copy-start.5
  536.2 2.5 copy-start.7
  541.2 9.9 %copy-start.3 = (bf16[768,384]{1,0:T(8,128)(2,1)S(1)}, bf16[768,384]{1,0:T(8,128)(2,1)}, u32[]{:S(2)}) copy-start(bf16[768,384]{1,0:T(8,128)(2,1)} %get-tuple-element.5) | copy-start | bytes 1769476
  547.7 13.8 %all-to-all-start.7 = ((bf16[64,4,3,512]{3,0,2,1:T(8,128)(2,1)}), bf16[64,4,3,512]{3,0,2,1:T(8,128)(2,1)S(1)}, u32[]{:S(2)}, u32[]{:S(2)}) async-start(bf16[64,4,3,512]{3,0,2,1:T(8,128)(2,1)} %copy.78), calls=%async_computation.7 | async-start | bytes 1572864 | tf_op jit(solution)/shard_map/all_to_all | solution.py:109
  553.7 0.7 copy-start.12
  561.6 0.7 copy-start.10
Sparse Core Ops, SparseCore 0:
  253.1 71.8 all-reduce.2
where the time goes:
time: 571 us; the launch traced here: 570 us
  waiting for transfers between devices  440 us (77%)
  starting transfers between devices  79.5 us (14%)
  local copies, waits for them, and re-layouts  17.1 us (3%)
  matrix products  17 us (3%)
  between operations  14.3 us (3%)
    all_to_all x1, waiting for transfers between devices, shards(): lax.all_to_all(back_sum, 'node', split_axis=2, concat_axis=0, tiled=True)  86.3 us
    all_to_all x1, waiting for transfers between devices, shards(): lax.all_to_all(twice_grads, 'node', split_axis=0, concat_axis=2, tiled=True)  86.3 us
    all_to_all x1, waiting for transfers between devices, shards(): lax.all_to_all(twice_rows, 'node', split_axis=0, concat_axis=2, tiled=True)  83.8 us
    all_to_all x1, waiting for transfers between devices, shards(): lax.all_to_all(out_sum, 'node', split_axis=2, concat_axis=0, tiled=True)  81 us
    psum x1, waiting for transfers between devices, shards(): lax.psum(up_part.astype(jnp.bfloat16), 'tp').astype(jnp.float32)  72 us
    all_to_all x1, starting transfers between devices, shards(): lax.all_to_all(twice_rows, 'node', split_axis=0, concat_axis=2, tiled=True)  29.1 us
    all_to_all x1, starting transfers between devices, shards(): lax.all_to_all(out_sum, 'node', split_axis=2, concat_axis=0, tiled=True)  23.6 us
  transfers between devices with their start and end apart: 9, of which 9 were waited for; matrix products, arithmetic and copies ran while one was open for 4% of the time, Pallas kernels for 0%

commit v1 on v0

v1 whole, which is shorter than its diff:
```python
import jax
import jax.numpy as jnp
from jax import lax
from jax.experimental import pallas as pl
from jax.experimental.pallas import tpu as pltpu
from jax.sharding import PartitionSpec as P

MESH = pl.DeviceIdType.MESH
F32 = jnp.float32
BF16 = jnp.bfloat16
CAP = 3
CHUNKS = 2

LAST = (((1,), (1,)), ((), ()))
FIRST = (((0,), (0,)), ((), ()))


def mm(a, b, dims=(((1,), (0,)), ((), ()))):
    return lax.dot_general(a, b, dims, preferred_element_type=F32)


def make_kernel(ring, n_local, n_tp, tok_rows, topk, feat, half):
    experts = ring * n_local
    per_chunk = ring // CHUNKS
    rows = per_chunk * CAP
    plane = 2 * n_local
    n_exp = n_local
    all_rows = plane * rows
    part = all_rows // n_tp
    plus = ring // 2 - 1
    minus = ring // 2
    deltas = [(dc, dl) for dl in range(n_local) for dc in range(2) if (dc, dl) != (0, 0)]

    def kernel(
        tok_ref, grd_ref, rt_ref, rw_ref, wg_hbm, wu_hbm, wd_hbm,
        mixed_ref, gtok_ref, gg_ref, gu_ref, gd_ref,
        wg, wu, wd, btok, bgrd, bmeta, sel_s, sel_w, sel, xg, parts, got, acts,
        acc_g, acc_u, acc_d, ob, rob, c_mix, c_back, s_mix, s_back, r_mix, r_back,
        w_sem, ag_send, ag_recv, y_send, y_recv, x_send, x_recv, a_send, a_recv,
        o_send, o_recv, rs_send, rs_recv, own_sem,
    ):
        node = lax.axis_index("node")
        l = lax.axis_index("local")
        j = lax.axis_index("tp")
        z, c = node // 2, node % 2
        slot = c * n_local + l
        up = (lax.rem(z + 1, ring) * 2 + c, l, j)
        down = (lax.rem(z + ring - 1, ring) * 2 + c, l, j)

        def mate(dc, dl):
            cc, ll = lax.rem(c + dc, 2), lax.rem(l + dl, n_local)
            return cc, ll, (z * 2 + cc, ll, j)

        def peer(dj):
            jj = lax.rem(j + dj, n_tp)
            return jj, (node, l, jj)

        loads = [
            pltpu.make_async_copy(src.at[0], dst, w_sem.at[i])
            for i, (src, dst) in enumerate(((wg_hbm, wg), (wu_hbm, wu), (wd_hbm, wd)))
        ]
        for load in loads:
            load.start()

        barrier = pltpu.get_barrier_semaphore()
        partners = [up, down]
        partners += [mate(dc, dl)[2] for dc, dl in deltas]
        partners += [peer(dj)[1] for dj in range(1, n_tp)]
        for who in partners:
            pl.semaphore_signal(barrier, inc=1, device_id=who, device_id_type=MESH)
        pl.semaphore_wait(barrier, len(partners))

        bufs = (btok, bgrd, bmeta)

        def hop(way, s, item, src=None):
            buf = bufs[item]
            if way == 0:
                a, b, who = 2 * s - 1, 2 * s + 1, up
            else:
                a, b, who = 2 * s, 2 * s + 2, down
            return pltpu.make_async_remote_copy(
                src_ref=buf.at[a] if src is None else src,
                dst_ref=buf.at[b],
                send_sem=ag_send.at[way, s, item],
                recv_sem=ag_recv.at[way, s, item],
                device_id=who,
                device_id_type=MESH,
            )

        for item, src in ((0, tok_ref), (1, grd_ref)):
            for way in range(2):
                hop(way, 0, item, src).start()
        btok[0] = tok_ref[...]
        bgrd[0] = grd_ref[...]

        lanes = lax.broadcasted_iota(jnp.int32, (tok_rows, experts), 1)
        named = jnp.zeros((tok_rows, experts), F32)
        weight = jnp.zeros((tok_rows, experts), F32)
        for k in range(topk):
            hit = rt_ref[:, k : k + 1] == lanes
            named = named + hit.astype(F32)
            weight = weight + jnp.where(hit, rw_ref[:, k : k + 1], 0.0)
        before = lax.broadcasted_iota(jnp.int32, (tok_rows, tok_rows), 0) > lax.broadcasted_iota(
            jnp.int32, (tok_rows, tok_rows), 1
        )
        rank = mm(before.astype(F32).astype(BF16), named.astype(BF16))
        t_index = lax.broadcasted_iota(jnp.int32, (tok_rows, experts), 0).astype(F32)
        lines = []
        for cap in range(CAP):
            here = jnp.where(rank == cap, named, 0.0)
            lines.append(jnp.sum(here * (t_index + 1.0), axis=0, keepdims=True) - 1.0)
        for cap in range(CAP):
            here = jnp.where(rank == cap, named, 0.0)
            lines.append(jnp.sum(here * weight, axis=0, keepdims=True))
        lines.append(jnp.zeros((2, experts), F32))
        bmeta[0] = jnp.concatenate(lines, axis=0)
        for way in range(2):
            hop(way, 0, 2, bmeta.at[0]).start()

        def relay(s, _):
            for item in range(3):
                for way in range(2):
                    hop(way, s - 1, item, bufs[item].at[0]).wait_recv()
                    hop(way, s, item).start()
            return 0

        def pick(h):
            base = h * per_chunk
            e_lane = lax.broadcasted_iota(jnp.int32, (per_chunk, experts), 1)
            q = lax.broadcasted_iota(jnp.int32, (per_chunk, 1), 0)
            wide = lax.broadcasted_iota(jnp.int32, (per_chunk, per_chunk * tok_rows), 1)
            for cap in range(CAP):
                idx_all = bmeta[base : base + per_chunk, cap, :]
                w_all = bmeta[base : base + per_chunk, CAP + cap, :]
                for i in range(n_exp):
                    mine = e_lane == z * n_exp + i
                    idx = jnp.sum(jnp.where(mine, idx_all, 0.0), axis=1, keepdims=True)
                    w = jnp.sum(jnp.where(mine, w_all, 0.0), axis=1, keepdims=True)
                    idx = idx.astype(jnp.int32)
                    target = jnp.where(idx >= 0, q * tok_rows + idx, -1)
                    at = i * rows + cap * per_chunk
                    sel_s[h, at : at + per_chunk, :] = (wide == target).astype(F32).astype(BF16)
                    sel_w[h, at : at + per_chunk, :] = jnp.broadcast_to(w, (per_chunk, 128))
            s = sel_s[h]
            x = mm(s, btok[base : base + per_chunk].reshape(per_chunk * tok_rows, feat))
            g = mm(s, bgrd[base : base + per_chunk].reshape(per_chunk * tok_rows, feat))
            g = g * sel_w[h][:, 0:1]
            for i in range(n_exp):
                sel[h, i, 0] = x[i * rows : (i + 1) * rows].astype(BF16)
                sel[h, i, 1] = g[i * rows : (i + 1) * rows].astype(BF16)

        def y_copy(h, d):
            dc, dl = deltas[d]
            cc, ll, who = mate(dc, dl)
            return pltpu.make_async_remote_copy(
                src_ref=sel.at[h, cc * 2 + ll // 2],
                dst_ref=xg.at[h, slot],
                send_sem=y_send.at[h, d],
                recv_sem=y_recv.at[h, d],
                device_id=who,
                device_id_type=MESH,
            )

        def y_arrival(h, d):
            dc, dl = deltas[d]
            cc, ll, who = mate(2 - dc, n_local - dl)
            return pltpu.make_async_remote_copy(
                src_ref=sel.at[h, 0],
                dst_ref=xg.at[h, cc * n_local + ll],
                send_sem=y_send.at[h, d],
                recv_sem=y_recv.at[h, d],
                device_id=who,
                device_id_type=MESH,
            )

        def y_out(h):
            for d in range(len(deltas)):
                y_copy(h, d).start()
            pltpu.make_async_copy(sel.at[h, c * 2 + l // 2], xg.at[h, slot], own_sem.at[h]).start()

        def x_copy(h, dj):
            jj, who = peer(dj)
            return pltpu.make_async_remote_copy(
                src_ref=parts.at[h, jj],
                dst_ref=got.at[h, dj - 1],
                send_sem=x_send.at[h, dj - 1],
                recv_sem=x_recv.at[h, dj - 1],
                device_id=who,
                device_id_type=MESH,
            )

        def first_matmuls(h):
            for d in range(len(deltas)):
                y_arrival(h, d).wait_recv()
            pltpu.make_async_copy(sel.at[h, c * 2 + l // 2], xg.at[h, slot], own_sem.at[h]).wait()
            x = xg[h, :, 0].reshape(all_rows, feat)
            g = xg[h, :, 1].reshape(all_rows, feat)
            parts[h, :, 0] = mm(x, wg[...]).astype(BF16).reshape(n_tp, part, half)
            parts[h, :, 1] = mm(x, wu[...]).astype(BF16).reshape(n_tp, part, half)
            parts[h, :, 2] = mm(g, wd[...], LAST).astype(BF16).reshape(n_tp, part, half)
            for dj in range(1, n_tp):
                x_copy(h, dj).start()

        def a_copy(h, dj, arrival=False):
            jj, who = peer(dj)
            at = lax.rem(j + n_tp - dj, n_tp) if arrival else j
            return pltpu.make_async_remote_copy(
                src_ref=acts.at[h, j],
                dst_ref=acts.at[h, at],
                send_sem=a_send.at[h, dj - 1],
                recv_sem=a_recv.at[h, dj - 1],
                device_id=who,
                device_id_type=MESH,
            )

        def activation(h):
            for dj in range(1, n_tp):
                x_copy(h, dj).wait_recv()
            total = []
            for kind in range(3):
                value = parts[h, j, kind].astype(F32)
                for dj in range(1, n_tp):
                    value = value + got[h, dj - 1, kind].astype(F32)
                total.append(value)
            gate, up_val, d_hidden = total
            sig = jax.nn.sigmoid(gate)
            act = gate * sig
            acts[h, j, 0] = (act * up_val).astype(BF16)
            acts[h, j, 1] = (d_hidden * up_val * sig * (1.0 + gate * (1.0 - sig))).astype(BF16)
            acts[h, j, 2] = (d_hidden * act).astype(BF16)
            for dj in range(1, n_tp):
                a_copy(h, dj).start()

        def o_copy(h, d):
            dc, dl = deltas[d]
            cc, ll, who = mate(dc, dl)
            return pltpu.make_async_remote_copy(
                src_ref=ob.at[h, cc * n_local + ll],
                dst_ref=rob.at[h, slot],
                send_sem=o_send.at[h, d],
                recv_sem=o_recv.at[h, d],
                device_id=who,
                device_id_type=MESH,
            )

        def o_arrival(h, d):
            dc, dl = deltas[d]
            cc, ll, who = mate(2 - dc, n_local - dl)
            return pltpu.make_async_remote_copy(
                src_ref=ob.at[h, 0],
                dst_ref=rob.at[h, cc * n_local + ll],
                send_sem=o_send.at[h, d],
                recv_sem=o_recv.at[h, d],
                device_id=who,
                device_id_type=MESH,
            )

        def own_out(h):
            return pltpu.make_async_copy(ob.at[h, slot], rob.at[h, slot], own_sem.at[CHUNKS + h])

        def last_matmuls(h):
            for dj in range(1, n_tp):
                a_copy(h, dj, True).wait_recv()
            hidden = acts[h, :, 0].reshape(all_rows, half)
            d_gate = acts[h, :, 1].reshape(all_rows, half)
            d_up = acts[h, :, 2].reshape(all_rows, half)
            ob[h, :, 0] = mm(hidden, wd[...]).astype(BF16).reshape(plane, rows, feat)
            back = mm(d_gate, wg[...], LAST) + mm(d_up, wu[...], LAST)
            ob[h, :, 1] = back.astype(BF16).reshape(plane, rows, feat)
            for d in range(len(deltas)):
                o_copy(h, d).start()
            own_out(h).start()

        def weight_grads(h):
            x = xg[h, :, 0].reshape(all_rows, feat)
            g = xg[h, :, 1].reshape(all_rows, feat)
            hidden = acts[h, :, 0].reshape(all_rows, half)
            d_gate = acts[h, :, 1].reshape(all_rows, half)
            d_up = acts[h, :, 2].reshape(all_rows, half)
            for acc, out, a, b in (
                (acc_d, gd_ref, hidden, g),
                (acc_g, gg_ref, x, d_gate),
                (acc_u, gu_ref, x, d_up),
            ):
                value = mm(a, b, FIRST)
                if h > 0:
                    value = acc[...] + value
                if h < CHUNKS - 1:
                    acc[...] = value
                else:
                    out[0] = value.astype(BF16)

        def contributions(h):
            for d in range(len(deltas)):
                o_arrival(h, d).wait_recv()
            own_out(h).wait()
            base = h * per_chunk
            s = sel_s[h]
            outs, backs = [], []
            for i in range(n_exp):
                for kind, keep in ((0, outs), (1, backs)):
                    value = rob[h, 2 * i, kind].astype(F32) + rob[h, 2 * i + 1, kind].astype(F32)
                    keep.append(value.astype(BF16))
            row_out = jnp.concatenate(outs, axis=0).astype(F32) * sel_w[h][:, 0:1]
            high = row_out.astype(BF16)
            low = (row_out - high.astype(F32)).astype(BF16)
            mix = mm(s, high, FIRST) + mm(s, low, FIRST)
            c_mix[base : base + per_chunk] = mix.reshape(per_chunk, tok_rows, feat)
            back = mm(s, jnp.concatenate(backs, axis=0), FIRST)
            c_back[base : base + per_chunk] = back.reshape(per_chunk, tok_rows, feat)

        lax.fori_loop(1, per_chunk // 2 + 1, relay, 0)
        pick(0)
        y_out(0)
        lax.fori_loop(per_chunk // 2 + 1, per_chunk // 2 + 6, relay, 0)
        for load in loads:
            load.wait()
        first_matmuls(0)
        lax.fori_loop(per_chunk // 2 + 6, plus, relay, 0)
        for item in range(3):
            hop(0, plus - 1, item).wait_recv()
            hop(0, plus, item).start()
            hop(1, plus - 1, item).wait_recv()
        for item in range(3):
            hop(0, plus, item).wait_recv()
        pick(1)
        y_out(1)
        activation(0)
        first_matmuls(1)
        last_matmuls(0)
        weight_grads(0)
        activation(1)
        contributions(0)
        last_matmuls(1)
        weight_grads(1)
        contributions(1)

        pieces = ((c_mix, s_mix, r_mix), (c_back, s_back, r_back))

        def fold(way, s, item):
            _, send, receive = pieces[item]
            return pltpu.make_async_remote_copy(
                src_ref=send.at[way, s],
                dst_ref=receive.at[way, s],
                send_sem=rs_send.at[way, s, item],
                recv_sem=rs_recv.at[way, s, item],
                device_id=up if way == 0 else down,
                device_id_type=MESH,
            )

        def place(way, s):
            return 2 * (plus - s) if way == 0 else 2 * (minus - s) - 1

        for way in range(2):
            for item in range(2):
                contrib, send, _ = pieces[item]
                send[way, 0] = contrib[place(way, 0)].astype(BF16)
                fold(way, 0, item).start()

        def add_on(way, s, item):
            contrib, send, receive = pieces[item]
            fold(way, s - 1, item).wait_recv()
            value = contrib[place(way, s)] + receive[way, s - 1].astype(F32)
            send[way, s] = value.astype(BF16)
            fold(way, s, item).start()

        def fold_step(s, _):
            for item in range(2):
                for way in range(2):
                    add_on(way, s, item)
            return 0

        lax.fori_loop(1, plus, fold_step, 0)
        for item in range(2):
            add_on(1, plus, item)
        for item, out in ((0, mixed_ref), (1, gtok_ref)):
            contrib, _, receive = pieces[item]
            fold(0, plus - 1, item).wait_recv()
            fold(1, minus - 1, item).wait_recv()
            value = contrib[0] + receive[0, plus - 1].astype(F32)
            value = value + receive[1, minus - 1].astype(F32)
            out[...] = value.astype(BF16)

        def drain(s, _):
            for item in range(3):
                for way in range(2):
                    hop(way, s, item, bufs[item].at[0]).wait_send()
            for item in range(2):
                for way in range(2):
                    fold(way, s, item).wait_send()
            return 0

        lax.fori_loop(0, plus, drain, 0)
        for item in range(3):
            hop(0, plus, item).wait_send()
        for item in range(2):
            fold(1, plus, item).wait_send()
        for h in range(CHUNKS):
            for d in range(len(deltas)):
                y_copy(h, d).wait_send()
                o_copy(h, d).wait_send()
            for dj in range(1, n_tp):
                x_copy(h, dj).wait_send()
                a_copy(h, dj).wait_send()

    scratch = [
        pltpu.VMEM((feat, half), BF16),
        pltpu.VMEM((feat, half), BF16),
        pltpu.VMEM((half, feat), BF16),
        pltpu.VMEM((ring, tok_rows, feat), BF16),
        pltpu.VMEM((ring, tok_rows, feat), BF16),
        pltpu.VMEM((ring, 8, experts), F32),
        pltpu.VMEM((CHUNKS, n_exp * rows, per_chunk * tok_rows), BF16),
        pltpu.VMEM((CHUNKS, n_exp * rows, 128), F32),
        pltpu.VMEM((CHUNKS, n_exp, 2, rows, feat), BF16),
        pltpu.VMEM((CHUNKS, plane, 2, rows, feat), BF16),
        pltpu.VMEM((CHUNKS, n_tp, 3, part, half), BF16),
        pltpu.VMEM((CHUNKS, n_tp - 1, 3, part, half), BF16),
        pltpu.VMEM((CHUNKS, n_tp, 3, part, half), BF16),
        pltpu.VMEM((feat, half), F32),
        pltpu.VMEM((feat, half), F32),
        pltpu.VMEM((half, feat), F32),
        pltpu.VMEM((CHUNKS, plane, 2, rows, feat), BF16),
        pltpu.VMEM((CHUNKS, plane, 2, rows, feat), BF16),
        pltpu.VMEM((ring, tok_rows, feat), F32),
        pltpu.VMEM((ring, tok_rows, feat), F32),
        pltpu.VMEM((2, minus, tok_rows, feat), BF16),
        pltpu.VMEM((2, minus, tok_rows, feat), BF16),
        pltpu.VMEM((2, minus, tok_rows, feat), BF16),
        pltpu.VMEM((2, minus, tok_rows, feat), BF16),
        pltpu.SemaphoreType.DMA((3,)),
        pltpu.SemaphoreType.DMA((2, minus, 3)),
        pltpu.SemaphoreType.DMA((2, minus, 3)),
        pltpu.SemaphoreType.DMA((CHUNKS, plane - 1)),
        pltpu.SemaphoreType.DMA((CHUNKS, plane - 1)),
        pltpu.SemaphoreType.DMA((CHUNKS, n_tp - 1)),
        pltpu.SemaphoreType.DMA((CHUNKS, n_tp - 1)),
        pltpu.SemaphoreType.DMA((CHUNKS, n_tp - 1)),
        pltpu.SemaphoreType.DMA((CHUNKS, n_tp - 1)),
        pltpu.SemaphoreType.DMA((CHUNKS, plane - 1)),
        pltpu.SemaphoreType.DMA((CHUNKS, plane - 1)),
        pltpu.SemaphoreType.DMA((2, minus, 2)),
        pltpu.SemaphoreType.DMA((2, minus, 2)),
        pltpu.SemaphoreType.DMA((2 * CHUNKS,)),
    ]
    return kernel, scratch


def solution(mesh):
    ring, n_local, n_tp = mesh.shape["node"] // 2, mesh.shape["local"], mesh.shape["tp"]

    def shards(tokens, grad_out, routes, route_weight, w_gate, w_up, w_down):
        tok_rows, feat = tokens.shape
        half = w_gate.shape[2]
        kernel, scratch = make_kernel(ring, n_local, n_tp, tok_rows, routes.shape[1], feat, half)
        vmem = pl.BlockSpec(memory_space=pltpu.VMEM)
        return pl.pallas_call(
            kernel,
            out_shape=(
                jax.ShapeDtypeStruct((tok_rows, feat), BF16),
                jax.ShapeDtypeStruct((tok_rows, feat), BF16),
                jax.ShapeDtypeStruct((1, feat, half), BF16),
                jax.ShapeDtypeStruct((1, feat, half), BF16),
                jax.ShapeDtypeStruct((1, half, feat), BF16),
            ),
            in_specs=[vmem] * 4 + [pl.BlockSpec(memory_space=pl.ANY)] * 3,
            out_specs=(vmem,) * 5,
            scratch_shapes=scratch,
            compiler_params=pltpu.CompilerParams(collective_id=0, has_side_effects=True),
            name="routed_experts",
        )(tokens, grad_out, routes, route_weight, w_gate, w_up, w_down)

    return jax.shard_map(
        shards,
        mesh=mesh,
        in_specs=(
            P(("node", "local"), "tp"),
            P(("node", "local"), "tp"),
            P(("node", "local"), None),
            P(("node", "local"), None),
            P(("node", "local"), "tp", None),
            P(("node", "local"), "tp", None),
            P(("node", "local"), None, "tp"),
        ),
        out_specs=(
            P(("node", "local"), "tp"),
            P(("node", "local"), "tp"),
            P(("node", "local"), "tp", None),
            P(("node", "local"), "tp", None),
            P(("node", "local"), None, "tp"),
        ),
        check_vma=False,
    )
```

time: 571 us -> 184 us (0.32)
  the two profiles are of different devices: /device:TPU:32 before, /device:TPU:2 now
where the time goes in v1:
time: 184 us
  Pallas kernels  175 us (95%)
  local copies, waits for them, and re-layouts  7.77 us (4%)
    pallas_call x1, Pallas kernels, shards(): pl.pallas_call(kernel, out_shape=(jax.ShapeDtypeStruct((tok_rows, feat),...  175 us
    unnamed x15, local copies, waits for them, and re-layouts  7.77 us

profile of v1, /device:TPU:2, one launch (start us, length us, event | category | flops | bytes accessed | tf_op | source)
XLA Modules:
  0.0 183.7 jit_solution(1531590035618179926)
XLA Ops:
  0.6 0.0 copy-start.3
  0.6 1.4 copy.12.rt_ref
  2.0 0.0 copy-done.3
  2.0 0.7 copy.13.rw_ref
  2.7 175.2 %routed_experts.1 = (bf16[32,512]{1,0:T(8,128)(2,1)}, bf16[32,512]{1,0:T(8,128)(2,1)}, bf16[1,512,384]{2,1,0:T(8,128)(2,1)}, bf16[1,512,384]{2,1,0:T(8,128)(2,1)}, bf16[1,384,512]{2,1,0:T(8,128)(2,1)}) custom-call(bf16[32,512]{1,0:T(8,128)(2,1)} %tok_ref.1, bf16[32,512]{1,0:T(8,128)(2,1)} %grd_ref.1, s32[32,8]{1,0:T(8,128)} %copy.12.rt_ref, ...), custom_call_target="tpu_custom_call" | custom-call | tf_op jit(solution)/shard_map/routed_experts/pallas_call | solution.py:457
  177.9 0.0 copy-start.2
  177.9 1.4 copy.19
  179.3 0.0 copy-done.2
  179.3 0.6 copy.20
  179.9 0.0 copy-start.1
  179.9 1.8 copy.21
  181.8 0.0 copy-done.1
  181.8 0.0 copy-start
  181.8 0.7 copy.22
  182.5 0.4 copy-done
  182.9 0.7 copy.23
Async XLA Ops:
  0.6 1.4 copy-start.3
  177.9 1.4 copy-start.2
  179.9 1.8 copy-start.1
  181.8 1.1 copy-start

commit v2 on v1

--- a/solution.py
+++ b/solution.py
@@ -27,25 +27,38 @@
     n_exp = n_local
     all_rows = plane * rows
     part = all_rows // n_tp
-    plus = ring // 2 - 1
-    minus = ring // 2
+    chain = ring // 4
+    half_chain = chain // 2
+
+    def even(e):
+        return e if e < chain else e + chain
+
+    def odd(way, a):
+        near = chain + way * half_chain + a
+        return near if a < half_chain else near + chain + half_chain
+
     deltas = [(dc, dl) for dl in range(n_local) for dc in range(2) if (dc, dl) != (0, 0)]
 
     def kernel(
         tok_ref, grd_ref, rt_ref, rw_ref, wg_hbm, wu_hbm, wd_hbm,
         mixed_ref, gtok_ref, gg_ref, gu_ref, gd_ref,
         wg, wu, wd, btok, bgrd, bmeta, sel_s, sel_w, sel, xg, parts, got, acts,
-        acc_g, acc_u, acc_d, ob, rob, c_mix, c_back, s_mix, s_back, r_mix, r_back,
+        acc_g, acc_u, acc_d, ob, rob, c_mix, c_back,
+        s_mix, s_back, r_mix, r_back, t_mix, t_back, n_mix, n_back, o_mix, o_back, o_g, o_u, o_d,
         w_sem, ag_send, ag_recv, y_send, y_recv, x_send, x_recv, a_send, a_recv,
-        o_send, o_recv, rs_send, rs_recv, own_sem,
+        o_send, o_recv, rs_send, rs_recv, own_sem, sh_send, sh_recv, ln_send, ln_recv,
     ):
         node = lax.axis_index("node")
         l = lax.axis_index("local")
         j = lax.axis_index("tp")
         z, c = node // 2, node % 2
         slot = c * n_local + l
-        up = (lax.rem(z + 1, ring) * 2 + c, l, j)
-        down = (lax.rem(z + ring - 1, ring) * 2 + c, l, j)
+
+        def along(step):
+            return (lax.rem(z + ring + step, ring) * 2 + c, l, j)
+
+        two = (along(2), along(-2))
+        one = (along(1), along(-1))
 
         def mate(dc, dl):
             cc, ll = lax.rem(c + dc, 2), lax.rem(l + dl, n_local)
@@ -63,7 +76,7 @@
             load.start()
 
         barrier = pltpu.get_barrier_semaphore()
-        partners = [up, down]
+        partners = [*two, *one]
         partners += [mate(dc, dl)[2] for dc, dl in deltas]
         partners += [peer(dj)[1] for dj in range(1, n_tp)]
         for who in partners:
@@ -72,34 +85,49 @@
 
         bufs = (btok, bgrd, bmeta)
 
+        def carried(way, s):
+            return even(0) if s == 0 else even(2 * s - 1 + way)
+
         def hop(way, s, item, src=None):
             buf = bufs[item]
-            if way == 0:
-                a, b, who = 2 * s - 1, 2 * s + 1, up
-            else:
-                a, b, who = 2 * s, 2 * s + 2, down
-            return pltpu.make_async_remote_copy(
-                src_ref=buf.at[a] if src is None else src,
-                dst_ref=buf.at[b],
+            return pltpu.make_async_remote_copy(
+                src_ref=buf.at[carried(way, s)] if src is None else src,
+                dst_ref=buf.at[even(2 * s + 1 + way)],
                 send_sem=ag_send.at[way, s, item],
                 recv_sem=ag_recv.at[way, s, item],
-                device_id=who,
+                device_id=two[way],
+                device_id_type=MESH,
+            )
+
+        def share(way, s, item, src=None):
+            buf = bufs[item]
+            return pltpu.make_async_remote_copy(
+                src_ref=buf.at[carried(way, s)] if src is None else src,
+                dst_ref=buf.at[odd(way, s)],
+                send_sem=sh_send.at[way, s, item],
+                recv_sem=sh_recv.at[way, s, item],
+                device_id=one[way],
                 device_id_type=MESH,
             )
 
         for item, src in ((0, tok_ref), (1, grd_ref)):
             for way in range(2):
                 hop(way, 0, item, src).start()
+        for item, src in ((0, tok_ref), (1, grd_ref)):
+            for way in range(2):
+                share(way, 0, item, src).start()
         btok[0] = tok_ref[...]
         bgrd[0] = grd_ref[...]
 
         lanes = lax.broadcasted_iota(jnp.int32, (tok_rows, experts), 1)
         named = jnp.zeros((tok_rows, experts), F32)
         weight = jnp.zeros((tok_rows, experts), F32)
+        rt = jnp.transpose(rt_ref[...].astype(F32)).astype(jnp.int32)
+        rw = jnp.transpose(rw_ref[...])
         for k in range(topk):
-            hit = rt_ref[:, k : k + 1] == lanes
+            hit = rt[:, k : k + 1] == lanes
             named = named + hit.astype(F32)
-            weight = weight + jnp.where(hit, rw_ref[:, k : k + 1], 0.0)
+            weight = weight + jnp.where(hit, rw[:, k : k + 1], 0.0)
         before = lax.broadcasted_iota(jnp.int32, (tok_rows, tok_rows), 0) > lax.broadcasted_iota(
             jnp.int32, (tok_rows, tok_rows), 1
         )
@@ -115,14 +143,26 @@
         lines.append(jnp.zeros((2, experts), F32))
         bmeta[0] = jnp.concatenate(lines, axis=0)
         for way in range(2):
-            hop(way, 0, 2, bmeta.at[0]).start()
-
-        def relay(s, _):
+            hop(way, 0, 2).start()
+            share(way, 0, 2).start()
+
+        def relay(s):
+            ways = [way for way in range(2) if way == 0 or s < chain]
             for item in range(3):
-                for way in range(2):
-                    hop(way, s - 1, item, bufs[item].at[0]).wait_recv()
-                    hop(way, s, item).start()
-            return 0
+                for way in ways:
+                    hop(way, s - 1, item).wait_recv()
+                    if s < chain - way:
+                        hop(way, s, item).start()
+            if s < chain:
+                for item in range(3):
+                    for way in range(2):
+                        share(way, s, item).start()
+
+        def shared(first, last):
+            for s in range(first, last):
+                for item in range(3):
+                    for way in range(2):
+                        share(way, s, item).wait_recv()
 
         def pick(h):
             base = h * per_chunk
@@ -278,9 +318,9 @@
             d_gate = acts[h, :, 1].reshape(all_rows, half)
             d_up = acts[h, :, 2].reshape(all_rows, half)
             for acc, out, a, b in (
-                (acc_d, gd_ref, hidden, g),
-                (acc_g, gg_ref, x, d_gate),
-                (acc_u, gu_ref, x, d_up),
+                (acc_d, o_d, hidden, g),
+                (acc_g, o_g, x, d_gate),
+                (acc_u, o_u, x, d_up),
             ):
                 value = mm(a, b, FIRST)
                 if h > 0:
@@ -288,7 +328,7 @@
                 if h < CHUNKS - 1:
                     acc[...] = value
                 else:
-                    out[0] = value.astype(BF16)
+                    out[...] = value.astype(BF16)
 
         def contributions(h):
             for d in range(len(deltas)):
@@ -309,20 +349,19 @@
             back = mm(s, jnp.concatenate(backs, axis=0), FIRST)
             c_back[base : base + per_chunk] = back.reshape(per_chunk, tok_rows, feat)
 
-        lax.fori_loop(1, per_chunk // 2 + 1, relay, 0)
+        for s in range(1, half_chain + 1):
+            relay(s)
+        shared(0, half_chain)
         pick(0)
         y_out(0)
-        lax.fori_loop(per_chunk // 2 + 1, per_chunk // 2 + 6, relay, 0)
+        for s in range(half_chain + 1, chain - 1):
+            relay(s)
         for load in loads:
             load.wait()
         first_matmuls(0)
-        lax.fori_loop(per_chunk // 2 + 6, plus, relay, 0)
-        for item in range(3):
-            hop(0, plus - 1, item).wait_recv()
-            hop(0, plus, item).start()
-            hop(1, plus - 1, item).wait_recv()
-        for item in range(3):
-            hop(0, plus, item).wait_recv()
+        for s in range(chain - 1, chain + 1):
+            relay(s)
+        shared(half_chain, chain)
         pick(1)
         y_out(1)
         activation(0)
@@ -333,68 +372,96 @@
         contributions(0)
         last_matmuls(1)
         weight_grads(1)
+        stores = [
+            pltpu.make_async_copy(src, dst.at[0], w_sem.at[3 + i])
+            for i, (src, dst) in enumerate(((o_g, gg_ref), (o_u, gu_ref), (o_d, gd_ref)))
+        ]
+        for store in stores:
+            store.start()
         contributions(1)
 
-        pieces = ((c_mix, s_mix, r_mix), (c_back, s_back, r_back))
+        pieces = (
+            (c_mix, s_mix, r_mix, t_mix, n_mix),
+            (c_back, s_back, r_back, t_back, n_back),
+        )
+
+        def lend(way, a, item):
+            _, _, _, send, receive = pieces[item]
+            return pltpu.make_async_remote_copy(
+                src_ref=send.at[way, a],
+                dst_ref=receive.at[way, a],
+                send_sem=ln_send.at[way, a, item],
+                recv_sem=ln_recv.at[way, a, item],
+                device_id=one[way],
+                device_id_type=MESH,
+            )
 
         def fold(way, s, item):
-            _, send, receive = pieces[item]
+            _, send, receive, _, _ = pieces[item]
             return pltpu.make_async_remote_copy(
                 src_ref=send.at[way, s],
                 dst_ref=receive.at[way, s],
                 send_sem=rs_send.at[way, s, item],
                 recv_sem=rs_recv.at[way, s, item],
-                device_id=up if way == 0 else down,
-                device_id_type=MESH,
-            )
-
-        def place(way, s):
-            return 2 * (plus - s) if way == 0 else 2 * (minus - s) - 1
-
-        for way in range(2):
-            for item in range(2):
-                contrib, send, _ = pieces[item]
-                send[way, 0] = contrib[place(way, 0)].astype(BF16)
-                fold(way, 0, item).start()
-
-        def add_on(way, s, item):
-            contrib, send, receive = pieces[item]
-            fold(way, s - 1, item).wait_recv()
-            value = contrib[place(way, s)] + receive[way, s - 1].astype(F32)
+                device_id=two[way],
+                device_id_type=MESH,
+            )
+
+        def lend_out(way, a, item):
+            contrib, _, _, send, _ = pieces[item]
+            send[way, a] = contrib[odd(1 - way, a)].astype(BF16)
+            lend(way, a, item).start()
+
+        def add_on(way, away, item):
+            contrib, send, receive, _, lent = pieces[item]
+            s = chain - away
+            value = contrib[even(2 * away - way)]
+            if away < chain:
+                lend(way, away, item).wait_recv()
+                value = value + lent[way, away].astype(F32)
+            if away < chain - 1 + way:
+                fold(way, s - 1, item).wait_recv()
+                value = value + receive[way, s - 1].astype(F32)
             send[way, s] = value.astype(BF16)
             fold(way, s, item).start()
 
-        def fold_step(s, _):
+        for item in range(2):
+            add_on(1, chain, item)
+        for a in range(chain - 1, -1, -1):
             for item in range(2):
                 for way in range(2):
-                    add_on(way, s, item)
-            return 0
-
-        lax.fori_loop(1, plus, fold_step, 0)
-        for item in range(2):
-            add_on(1, plus, item)
-        for item, out in ((0, mixed_ref), (1, gtok_ref)):
-            contrib, _, receive = pieces[item]
-            fold(0, plus - 1, item).wait_recv()
-            fold(1, minus - 1, item).wait_recv()
-            value = contrib[0] + receive[0, plus - 1].astype(F32)
-            value = value + receive[1, minus - 1].astype(F32)
+                    lend_out(way, a, item)
+            if a < chain - 1:
+                for item in range(2):
+                    for way in range(2):
+                        add_on(way, a + 1, item)
+        for item, out in ((0, o_mix), (1, o_back)):
+            contrib, _, receive, _, lent = pieces[item]
+            value = contrib[0]
+            for way in range(2):
+                lend(way, 0, item).wait_recv()
+                value = value + lent[way, 0].astype(F32)
+                fold(way, chain - 1, item).wait_recv()
+                value = value + receive[way, chain - 1].astype(F32)
             out[...] = value.astype(BF16)
-
-        def drain(s, _):
+        stores += [
+            pltpu.make_async_copy(o_mix, mixed_ref, w_sem.at[6]),
+            pltpu.make_async_copy(o_back, gtok_ref, w_sem.at[7]),
+        ]
+        for store in stores[3:]:
+            store.start()
+
+        for s in range(chain):
             for item in range(3):
                 for way in range(2):
-                    hop(way, s, item, bufs[item].at[0]).wait_send()
+                    share(way, s, item).wait_send()
+                    if s < chain - way:
+                        hop(way, s, item).wait_send()
             for item in range(2):
                 for way in range(2):
-                    fold(way, s, item).wait_send()
-            return 0
-
-        lax.fori_loop(0, plus, drain, 0)
-        for item in range(3):
-            hop(0, plus, item).wait_send()
-        for item in range(2):
-            fold(1, plus, item).wait_send()
+                    lend(way, s, item).wait_send()
+                    if s > 0 or way == 1:
+                        fold(way, s, item).wait_send()
         for h in range(CHUNKS):
             for d in range(len(deltas)):
                 y_copy(h, d).wait_send()
@@ -402,6 +469,8 @@
             for dj in range(1, n_tp):
                 x_copy(h, dj).wait_send()
                 a_copy(h, dj).wait_send()
+        for store in stores:
+            store.wait()
 
     scratch = [
         pltpu.VMEM((feat, half), BF16),
@@ -424,13 +493,15 @@
         pltpu.VMEM((CHUNKS, plane, 2, rows, feat), BF16),
         pltpu.VMEM((ring, tok_rows, feat), F32),
         pltpu.VMEM((ring, tok_rows, feat), F32),
-        pltpu.VMEM((2, minus, tok_rows, feat), BF16),
-        pltpu.VMEM((2, minus, tok_rows, feat), BF16),
-        pltpu.VMEM((2, minus, tok_rows, feat), BF16),
-        pltpu.VMEM((2, minus, tok_rows, feat), BF16),
-        pltpu.SemaphoreType.DMA((3,)),
-        pltpu.SemaphoreType.DMA((2, minus, 3)),
-        pltpu.SemaphoreType.DMA((2, minus, 3)),
+        *[pltpu.VMEM((2, chain, tok_rows, feat), BF16)] * 8,
+        pltpu.VMEM((tok_rows, feat), BF16),
+        pltpu.VMEM((tok_rows, feat), BF16),
+        pltpu.VMEM((feat, half), BF16),
+        pltpu.VMEM((feat, half), BF16),
+        pltpu.VMEM((half, feat), BF16),
+        pltpu.SemaphoreType.DMA((8,)),
+        pltpu.SemaphoreType.DMA((2, chain, 3)),
+        pltpu.SemaphoreType.DMA((2, chain, 3)),
         pltpu.SemaphoreType.DMA((CHUNKS, plane - 1)),
         pltpu.SemaphoreType.DMA((CHUNKS, plane - 1)),
         pltpu.SemaphoreType.DMA((CHUNKS, n_tp - 1)),
@@ -439,11 +510,43 @@
         pltpu.SemaphoreType.DMA((CHUNKS, n_tp - 1)),
         pltpu.SemaphoreType.DMA((CHUNKS, plane - 1)),
         pltpu.SemaphoreType.DMA((CHUNKS, plane - 1)),
-        pltpu.SemaphoreType.DMA((2, minus, 2)),
-        pltpu.SemaphoreType.DMA((2, minus, 2)),
+        pltpu.SemaphoreType.DMA((2, chain, 2)),
+        pltpu.SemaphoreType.DMA((2, chain, 2)),
         pltpu.SemaphoreType.DMA((2 * CHUNKS,)),
+        pltpu.SemaphoreType.DMA((2, chain, 3)),
+        pltpu.SemaphoreType.DMA((2, chain, 3)),
+        pltpu.SemaphoreType.DMA((2, chain, 2)),
+        pltpu.SemaphoreType.DMA((2, chain, 2)),
     ]
     return kernel, scratch
+
+
+def deliver(arrays):
+    count = len(arrays)
+
+    def kernel(*refs):
+        sources, targets, held = refs[:count], refs[count : 2 * count], refs[2 * count : 3 * count]
+        in_sem, out_sem = refs[3 * count :]
+        loads = [pltpu.make_async_copy(sources[i], held[i], in_sem.at[i]) for i in range(count)]
+        stores = [pltpu.make_async_copy(held[i], targets[i], out_sem.at[i]) for i in range(count)]
+        for load in loads:
+            load.start()
+        for load, store in zip(loads, stores):
+            load.wait()
+            store.start()
+        for store in stores:
+            store.wait()
+
+    anywhere = pl.BlockSpec(memory_space=pl.ANY)
+    return pl.pallas_call(
+        kernel,
+        out_shape=tuple(jax.ShapeDtypeStruct(a.shape, a.dtype) for a in arrays),
+        in_specs=[anywhere] * count,
+        out_specs=(anywhere,) * count,
+        scratch_shapes=[pltpu.VMEM(a.shape, a.dtype) for a in arrays]
+        + [pltpu.SemaphoreType.DMA((count,))] * 2,
+        name="deliver",
+    )(*arrays)
 
 
 def solution(mesh):
@@ -454,7 +557,7 @@
         half = w_gate.shape[2]
         kernel, scratch = make_kernel(ring, n_local, n_tp, tok_rows, routes.shape[1], feat, half)
         vmem = pl.BlockSpec(memory_space=pltpu.VMEM)
-        return pl.pallas_call(
+        outs = pl.pallas_call(
             kernel,
             out_shape=(
                 jax.ShapeDtypeStruct((tok_rows, feat), BF16),
@@ -464,11 +567,12 @@
                 jax.ShapeDtypeStruct((1, half, feat), BF16),
             ),
             in_specs=[vmem] * 4 + [pl.BlockSpec(memory_space=pl.ANY)] * 3,
-            out_specs=(vmem,) * 5,
+            out_specs=(pl.BlockSpec(memory_space=pl.ANY),) * 5,
             scratch_shapes=scratch,
             compiler_params=pltpu.CompilerParams(collective_id=0, has_side_effects=True),
             name="routed_experts",
-        )(tokens, grad_out, routes, route_weight, w_gate, w_up, w_down)
+        )(tokens, grad_out, routes.T, route_weight.T, w_gate, w_up, w_down)
+        return deliver(outs)
 
     return jax.shard_map(
         shards,

time: 184 us -> 154 us (0.84)
  the two profiles are of different devices: /device:TPU:2 before, /device:TPU:32 now
where the time goes in v2:
time: 154 us
  Pallas kernels  153 us (99%)
    pallas_call x1, Pallas kernels, shards(): pl.pallas_call(kernel, out_shape=(jax.ShapeDtypeStruct((tok_rows, feat),...  151 us

profile of v2, /device:TPU:32, one launch (start us, length us, event | category | flops | bytes accessed | tf_op | source)
XLA Modules:
  0.0 153.8 jit_solution(15146742848506943202)
XLA Ops:
  0.6 151.1 %routed_experts.1 = (bf16[32,512]{1,0:T(8,128)(2,1)}, bf16[32,512]{1,0:T(8,128)(2,1)}, bf16[1,512,384]{2,1,0:T(8,128)(2,1)}, bf16[1,512,384]{2,1,0:T(8,128)(2,1)}, bf16[1,384,512]{2,1,0:T(8,128)(2,1)}) custom-call(bf16[32,512]{1,0:T(8,128)(2,1)} %tok_ref.1, bf16[32,512]{1,0:T(8,128)(2,1)} %grd_ref.1, s32[8,32]{1,0:T(8,128)} %bitcast.2, f32[8,32]{1,0:T(8,128)} %bitcast.3, ...), custom_call_target="tpu_custom_call" | custom-call | tf_op jit(solution)/shard_map/routed_experts/pallas_call | solution.py:560
  151.7 2.1 %deliver.1 = (bf16[32,512]{1,0:T(8,128)(2,1)}, bf16[32,512]{1,0:T(8,128)(2,1)}, bf16[1,512,384]{2,1,0:T(8,128)(2,1)}, bf16[1,512,384]{2,1,0:T(8,128)(2,1)}, bf16[1,384,512]{2,1,0:T(8,128)(2,1)}) custom-call(bf16[32,512]{1,0:T(8,128)(2,1)} %get-tuple-element.10.refs_0_, bf16[32,512]{1,0:T(8,128)(2,1)} %get-tuple-element.11.refs_1_, ...), custom_call_target="tpu_custom_call" | custom-call | tf_op jit(solution)/shard_map/deliver/pallas_call | solution.py:541

commit v3 on v2

--- a/solution.py
+++ b/solution.py
@@ -9,7 +9,10 @@
 F32 = jnp.float32
 BF16 = jnp.bfloat16
 CAP = 3
-CHUNKS = 2
+CHUNKS = 4
+
+SHARED = 16
+PARTS = 2
 
 LAST = (((1,), (1,)), ((), ()))
 FIRST = (((0,), (0,)), ((), ()))
@@ -26,17 +29,19 @@
     plane = 2 * n_local
     n_exp = n_local
     all_rows = plane * rows
-    part = all_rows // n_tp
+    strip = all_rows // n_tp
     chain = ring // 4
-    half_chain = chain // 2
+
+    quarter = chain // 4
 
     def even(e):
-        return e if e < chain else e + chain
+        return e // (2 * quarter) * per_chunk + e % (2 * quarter)
 
     def odd(way, a):
-        near = chain + way * half_chain + a
-        return near if a < half_chain else near + chain + half_chain
-
+        return a // quarter * per_chunk + 2 * quarter + way * quarter + a % quarter
+
+    piece = tok_rows // PARTS
+    legs = [(item, part) for item in range(2) for part in range(PARTS)] + [(2, 0)]
     deltas = [(dc, dl) for dl in range(n_local) for dc in range(2) if (dc, dl) != (0, 0)]
 
     def kernel(
@@ -46,7 +51,7 @@
         acc_g, acc_u, acc_d, ob, rob, c_mix, c_back,
         s_mix, s_back, r_mix, r_back, t_mix, t_back, n_mix, n_back, o_mix, o_back, o_g, o_u, o_d,
         w_sem, ag_send, ag_recv, y_send, y_recv, x_send, x_recv, a_send, a_recv,
-        o_send, o_recv, rs_send, rs_recv, own_sem, sh_send, sh_recv, ln_send, ln_recv,
+        o_send, o_recv, rs_send, rs_recv, own_sem, s_odd, lent_rows, odd_rows, sh_send, sh_recv, ln_send, ln_recv,
     ):
         node = lax.axis_index("node")
         l = lax.axis_index("local")
@@ -81,41 +86,70 @@
         partners += [peer(dj)[1] for dj in range(1, n_tp)]
         for who in partners:
             pl.semaphore_signal(barrier, inc=1, device_id=who, device_id_type=MESH)
-        pl.semaphore_wait(barrier, len(partners))
 
         bufs = (btok, bgrd, bmeta)
 
         def carried(way, s):
-            return even(0) if s == 0 else even(2 * s - 1 + way)
-
-        def hop(way, s, item, src=None):
-            buf = bufs[item]
-            return pltpu.make_async_remote_copy(
-                src_ref=buf.at[carried(way, s)] if src is None else src,
-                dst_ref=buf.at[even(2 * s + 1 + way)],
-                send_sem=ag_send.at[way, s, item],
-                recv_sem=ag_recv.at[way, s, item],
+            return 0 if s == 0 else 2 * s - 1 + way
+
+        def block(item, e):
+            return bmeta.at[even(e)] if item == 2 else bufs[item].at[e]
+
+        def cut(ref, part):
+            return ref.at[pl.ds(part * piece, piece)]
+
+        def hop(way, s, leg, first=None):
+            item, part = legs[leg]
+            src = block(item, carried(way, s)) if first is None else first
+            dst = block(item, 2 * s + 1 + way)
+            if item < 2:
+                src, dst = cut(src, part), cut(dst, part)
+            return pltpu.make_async_remote_copy(
+                src_ref=src,
+                dst_ref=dst,
+                send_sem=ag_send.at[item],
+                recv_sem=ag_recv.at[way, s, leg],
                 device_id=two[way],
                 device_id_type=MESH,
             )
 
-        def share(way, s, item, src=None):
-            buf = bufs[item]
-            return pltpu.make_async_remote_copy(
-                src_ref=buf.at[carried(way, s)] if src is None else src,
-                dst_ref=buf.at[odd(way, s)],
-                send_sem=sh_send.at[way, s, item],
+        def share(way, s, item):
+            if item == 2:
+                src, dst = block(2, carried(way, s)), bmeta.at[odd(way, s)]
+            else:
+                src = lent_rows.at[item, way, s]
+                dst = odd_rows.at[item, s // quarter, way * quarter + s % quarter]
+            return pltpu.make_async_remote_copy(
+                src_ref=src,
+                dst_ref=dst,
+                send_sem=sh_send.at[item],
                 recv_sem=sh_recv.at[way, s, item],
                 device_id=one[way],
                 device_id_type=MESH,
             )
 
-        for item, src in ((0, tok_ref), (1, grd_ref)):
+        def share_out(s):
             for way in range(2):
-                hop(way, 0, item, src).start()
-        for item, src in ((0, tok_ref), (1, grd_ref)):
+                share(way, s, 2).start()
             for way in range(2):
-                share(way, 0, item, src).start()
+                e = carried(way, s)
+                theirs = lax.rem(z + ring + (1, -1)[way], ring) * n_exp
+                meta = bmeta[even(e)]
+                r = lax.broadcasted_iota(jnp.int32, (SHARED, experts), 0)
+                lane = lax.broadcasted_iota(jnp.int32, (SHARED, experts), 1)
+                value = jnp.full((SHARED, experts), -1.0, F32)
+                target = jnp.full((SHARED, experts), -1, jnp.int32)
+                for cap in range(CAP):
+                    inside = (r >= cap * n_exp) & (r < (cap + 1) * n_exp)
+                    value = jnp.where(inside, meta[cap : cap + 1, :], value)
+                    target = jnp.where(inside, theirs + r - cap * n_exp, target)
+                idx = jnp.sum(jnp.where(lane == target, value + 1.0, 0.0), axis=1, keepdims=True) - 1.0
+                t_lane = lax.broadcasted_iota(jnp.int32, (SHARED, tok_rows), 1)
+                choose = (t_lane == idx.astype(jnp.int32)).astype(F32).astype(BF16)
+                for item in range(2):
+                    lent_rows[item, way, s] = mm(choose, bufs[item][e]).astype(BF16)
+                    share(way, s, item).start()
+
         btok[0] = tok_ref[...]
         bgrd[0] = grd_ref[...]
 
@@ -142,21 +176,30 @@
             lines.append(jnp.sum(here * weight, axis=0, keepdims=True))
         lines.append(jnp.zeros((2, experts), F32))
         bmeta[0] = jnp.concatenate(lines, axis=0)
+        for cap in range(CAP):
+            for i in range(n_exp):
+                q = lax.broadcasted_iota(jnp.int32, (per_chunk, 1), 0) - 2 * quarter
+                wide = lax.broadcasted_iota(jnp.int32, (per_chunk, 2 * quarter * SHARED), 1)
+                target = jnp.where(q >= 0, q * SHARED + cap * n_exp + i, -1)
+                at = i * rows + cap * per_chunk
+                s_odd[at : at + per_chunk, :] = (wide == target).astype(F32).astype(BF16)
+        pl.semaphore_wait(barrier, len(partners))
+        for leg, (item, _) in enumerate(legs[:-1]):
+            for way in range(2):
+                hop(way, 0, leg, (tok_ref, grd_ref)[item]).start()
         for way in range(2):
-            hop(way, 0, 2).start()
-            share(way, 0, 2).start()
+            hop(way, 0, len(legs) - 1).start()
+        share_out(0)
 
         def relay(s):
             ways = [way for way in range(2) if way == 0 or s < chain]
-            for item in range(3):
+            for leg in range(len(legs)):
                 for way in ways:
-                    hop(way, s - 1, item).wait_recv()
+                    hop(way, s - 1, leg).wait_recv()
                     if s < chain - way:
-                        hop(way, s, item).start()
+                        hop(way, s, leg).start()
             if s < chain:
-                for item in range(3):
-                    for way in range(2):
-                        share(way, s, item).start()
+                share_out(s)
 
         def shared(first, last):
             for s in range(first, last):
@@ -182,8 +225,14 @@
                     sel_s[h, at : at + per_chunk, :] = (wide == target).astype(F32).astype(BF16)
                     sel_w[h, at : at + per_chunk, :] = jnp.broadcast_to(w, (per_chunk, 128))
             s = sel_s[h]
-            x = mm(s, btok[base : base + per_chunk].reshape(per_chunk * tok_rows, feat))
-            g = mm(s, bgrd[base : base + per_chunk].reshape(per_chunk * tok_rows, feat))
+            near = s_odd[...]
+            evens = 2 * quarter
+            s = s[:, : evens * tok_rows]
+            x, g = [
+                mm(s, bufs[item][h * evens : (h + 1) * evens].reshape(evens * tok_rows, feat))
+                + mm(near, odd_rows[item, h].reshape(evens * SHARED, feat))
+                for item in range(2)
+            ]
             g = g * sel_w[h][:, 0:1]
             for i in range(n_exp):
                 sel[h, i, 0] = x[i * rows : (i + 1) * rows].astype(BF16)
@@ -195,7 +244,7 @@
             return pltpu.make_async_remote_copy(
                 src_ref=sel.at[h, cc * 2 + ll // 2],
                 dst_ref=xg.at[h, slot],
-                send_sem=y_send.at[h, d],
+                send_sem=y_send.at[h],
                 recv_sem=y_recv.at[h, d],
                 device_id=who,
                 device_id_type=MESH,
@@ -207,7 +256,7 @@
             return pltpu.make_async_remote_copy(
                 src_ref=sel.at[h, 0],
                 dst_ref=xg.at[h, cc * n_local + ll],
-                send_sem=y_send.at[h, d],
+                send_sem=y_send.at[h],
                 recv_sem=y_recv.at[h, d],
                 device_id=who,
                 device_id_type=MESH,
@@ -223,7 +272,7 @@
             return pltpu.make_async_remote_copy(
                 src_ref=parts.at[h, jj],
                 dst_ref=got.at[h, dj - 1],
-                send_sem=x_send.at[h, dj - 1],
+                send_sem=x_send.at[h],
                 recv_sem=x_recv.at[h, dj - 1],
                 device_id=who,
                 device_id_type=MESH,
@@ -235,9 +284,9 @@
             pltpu.make_async_copy(sel.at[h, c * 2 + l // 2], xg.at[h, slot], own_sem.at[h]).wait()
             x = xg[h, :, 0].reshape(all_rows, feat)
             g = xg[h, :, 1].reshape(all_rows, feat)
-            parts[h, :, 0] = mm(x, wg[...]).astype(BF16).reshape(n_tp, part, half)
-            parts[h, :, 1] = mm(x, wu[...]).astype(BF16).reshape(n_tp, part, half)
-            parts[h, :, 2] = mm(g, wd[...], LAST).astype(BF16).reshape(n_tp, part, half)
+            parts[h, :, 0] = mm(x, wg[...]).astype(BF16).reshape(n_tp, strip, half)
+            parts[h, :, 1] = mm(x, wu[...]).astype(BF16).reshape(n_tp, strip, half)
+            parts[h, :, 2] = mm(g, wd[...], LAST).astype(BF16).reshape(n_tp, strip, half)
             for dj in range(1, n_tp):
                 x_copy(h, dj).start()
 
@@ -247,7 +296,7 @@
             return pltpu.make_async_remote_copy(
                 src_ref=acts.at[h, j],
                 dst_ref=acts.at[h, at],
-                send_sem=a_send.at[h, dj - 1],
+                send_sem=a_send.at[h],
                 recv_sem=a_recv.at[h, dj - 1],
                 device_id=who,
                 device_id_type=MESH,
@@ -277,7 +326,7 @@
             return pltpu.make_async_remote_copy(
                 src_ref=ob.at[h, cc * n_local + ll],
                 dst_ref=rob.at[h, slot],
-                send_sem=o_send.at[h, d],
+                send_sem=o_send.at[h],
                 recv_sem=o_recv.at[h, d],
                 device_id=who,
                 device_id_type=MESH,
@@ -289,7 +338,7 @@
             return pltpu.make_async_remote_copy(
                 src_ref=ob.at[h, 0],
                 dst_ref=rob.at[h, cc * n_local + ll],
-                send_sem=o_send.at[h, d],
+                send_sem=o_send.at[h],
                 recv_sem=o_recv.at[h, d],
                 device_id=who,
                 device_id_type=MESH,
@@ -349,99 +398,137 @@
             back = mm(s, jnp.concatenate(backs, axis=0), FIRST)
             c_back[base : base + per_chunk] = back.reshape(per_chunk, tok_rows, feat)
 
-        for s in range(1, half_chain + 1):
+        def gathered(h):
+            shared(quarter * h, quarter * (h + 1))
+            pick(h)
+            y_out(h)
+
+        pieces = (
+            (c_mix, s_mix, r_mix, t_mix, n_mix),
+            (c_back, s_back, r_back, t_back, n_back),
+        )
+
+        def lend(way, a, item):
+            _, _, _, send, receive = pieces[item]
+            return pltpu.make_async_remote_copy(
+                src_ref=send.at[way, a],
+                dst_ref=receive.at[way, a],
+                send_sem=ln_send.at[item],
+                recv_sem=ln_recv.at[way, a, item],
+                device_id=one[way],
+                device_id_type=MESH,
+            )
+
+        def fold(way, s, item, part):
+            _, send, receive, _, _ = pieces[item]
+            return pltpu.make_async_remote_copy(
+                src_ref=cut(send.at[way, s], part),
+                dst_ref=cut(receive.at[way, s], part),
+                send_sem=rs_send.at[item],
+                recv_sem=rs_recv.at[way, s, item, part],
+                device_id=two[way],
+                device_id_type=MESH,
+            )
+
+        def lend_out(way, a, item):
+            contrib, _, _, send, _ = pieces[item]
+            send[way, a] = contrib[odd(1 - way, a)].astype(BF16)
+            lend(way, a, item).start()
+
+        def add_on(way, away, item):
+            contrib, send, receive, _, lent = pieces[item]
+            s = chain - away
+            if away < chain:
+                lend(way, away, item).wait_recv()
+            for part in range(PARTS):
+                at = pl.ds(part * piece, piece)
+                value = contrib[even(2 * away - way), at]
+                if away < chain:
+                    value = value + lent[way, away, at].astype(F32)
+                if away < chain - 1 + way:
+                    fold(way, s - 1, item, part).wait_recv()
+                    value = value + receive[way, s - 1, at].astype(F32)
+                send[way, s, at] = value.astype(BF16)
+                fold(way, s, item, part).start()
+
+        def returned(h):
+            contributions(h)
+            if h == CHUNKS - 1:
+                for item in range(2):
+                    add_on(1, chain, item)
+            for a in range(quarter * (h + 1) - 1, quarter * h - 1, -1):
+                for item in range(2):
+                    for way in range(2):
+                        lend_out(way, a, item)
+
+        for s in range(1, chain + 1):
             relay(s)
-        shared(0, half_chain)
-        pick(0)
-        y_out(0)
-        for s in range(half_chain + 1, chain - 1):
-            relay(s)
-        for load in loads:
-            load.wait()
-        first_matmuls(0)
-        for s in range(chain - 1, chain + 1):
-            relay(s)
-        shared(half_chain, chain)
-        pick(1)
-        y_out(1)
-        activation(0)
-        first_matmuls(1)
+            if s == 2:
+                gathered(0)
+            if s == 4:
+                gathered(1)
+                for load in loads:
+                    load.wait()
+                first_matmuls(0)
+            if s == 6:
+                gathered(2)
+                activation(0)
+                first_matmuls(1)
+        gathered(3)
+        first_matmuls(2)
+        activation(1)
         last_matmuls(0)
+        first_matmuls(3)
+        activation(2)
+        last_matmuls(1)
         weight_grads(0)
-        activation(1)
-        contributions(0)
-        last_matmuls(1)
+        activation(3)
+        returned(0)
+        last_matmuls(2)
         weight_grads(1)
+        returned(1)
+        last_matmuls(3)
+        weight_grads(2)
+        weight_grads(3)
         stores = [
             pltpu.make_async_copy(src, dst.at[0], w_sem.at[3 + i])
             for i, (src, dst) in enumerate(((o_g, gg_ref), (o_u, gu_ref), (o_d, gd_ref)))
         ]
         for store in stores:
             store.start()
-        contributions(1)
-
-        pieces = (
-            (c_mix, s_mix, r_mix, t_mix, n_mix),
-            (c_back, s_back, r_back, t_back, n_back),
-        )
-
-        def lend(way, a, item):
-            _, _, _, send, receive = pieces[item]
-            return pltpu.make_async_remote_copy(
-                src_ref=send.at[way, a],
-                dst_ref=receive.at[way, a],
-                send_sem=ln_send.at[way, a, item],
-                recv_sem=ln_recv.at[way, a, item],
-                device_id=one[way],
-                device_id_type=MESH,
-            )
-
-        def fold(way, s, item):
-            _, send, receive, _, _ = pieces[item]
-            return pltpu.make_async_remote_copy(
-                src_ref=send.at[way, s],
-                dst_ref=receive.at[way, s],
-                send_sem=rs_send.at[way, s, item],
-                recv_sem=rs_recv.at[way, s, item],
-                device_id=two[way],
-                device_id_type=MESH,
-            )
-
-        def lend_out(way, a, item):
-            contrib, _, _, send, _ = pieces[item]
-            send[way, a] = contrib[odd(1 - way, a)].astype(BF16)
-            lend(way, a, item).start()
-
-        def add_on(way, away, item):
-            contrib, send, receive, _, lent = pieces[item]
-            s = chain - away
-            value = contrib[even(2 * away - way)]
-            if away < chain:
-                lend(way, away, item).wait_recv()
-                value = value + lent[way, away].astype(F32)
-            if away < chain - 1 + way:
-                fold(way, s - 1, item).wait_recv()
-                value = value + receive[way, s - 1].astype(F32)
-            send[way, s] = value.astype(BF16)
-            fold(way, s, item).start()
-
-        for item in range(2):
-            add_on(1, chain, item)
-        for a in range(chain - 1, -1, -1):
+        returned(2)
+        returned(3)
+
+        for a in range(chain - 1, 0, -1):
             for item in range(2):
                 for way in range(2):
-                    lend_out(way, a, item)
-            if a < chain - 1:
-                for item in range(2):
-                    for way in range(2):
-                        add_on(way, a + 1, item)
+                    add_on(way, a, item)
+
+        def sent(ref, sem):
+            pltpu.make_async_remote_copy(
+                src_ref=ref, dst_ref=ref, send_sem=sem, recv_sem=own_sem.at[0],
+                device_id=two[0], device_id_type=MESH,
+            ).wait_send()
+
+        for h in range(CHUNKS):
+            sent(xg.at[h, pl.ds(0, plane - 1)], y_send.at[h])
+            sent(ob.at[h, pl.ds(0, plane - 1)], o_send.at[h])
+            sent(parts.at[h, pl.ds(0, n_tp - 1)], x_send.at[h])
+            sent(acts.at[h, pl.ds(0, n_tp - 1)], a_send.at[h])
+        for item in range(2):
+            sent(bufs[item].at[pl.ds(0, 2 * chain - 1)], ag_send.at[item])
+            sent(lent_rows.at[item], sh_send.at[item])
+            sent(pieces[item][3], ln_send.at[item])
+        sent(bmeta.at[pl.ds(0, 2 * chain - 1)], ag_send.at[2])
+        sent(bmeta.at[pl.ds(0, 2 * chain)], sh_send.at[2])
         for item, out in ((0, o_mix), (1, o_back)):
             contrib, _, receive, _, lent = pieces[item]
             value = contrib[0]
             for way in range(2):
                 lend(way, 0, item).wait_recv()
                 value = value + lent[way, 0].astype(F32)
-                fold(way, chain - 1, item).wait_recv()
+                for part in range(PARTS):
+                    fold(way, chain - 1, item, part).wait_recv()
                 value = value + receive[way, chain - 1].astype(F32)
             out[...] = value.astype(BF16)
         stores += [
@@ -451,24 +538,8 @@
         for store in stores[3:]:
             store.start()
 
-        for s in range(chain):
-            for item in range(3):
-                for way in range(2):
-                    share(way, s, item).wait_send()
-                    if s < chain - way:
-                        hop(way, s, item).wait_send()
-            for item in range(2):
-                for way in range(2):
-                    lend(way, s, item).wait_send()
-                    if s > 0 or way == 1:
-                        fold(way, s, item).wait_send()
-        for h in range(CHUNKS):
-            for d in range(len(deltas)):
-                y_copy(h, d).wait_send()
-                o_copy(h, d).wait_send()
-            for dj in range(1, n_tp):
-                x_copy(h, dj).wait_send()
-                a_copy(h, dj).wait_send()
+        for item in range(2):
+            sent(bufs[item].at[pl.ds(0, 2 * chain - 1)], rs_send.at[item])
         for store in stores:
             store.wait()
 
@@ -476,16 +547,16 @@
         pltpu.VMEM((feat, half), BF16),
         pltpu.VMEM((feat, half), BF16),
         pltpu.VMEM((half, feat), BF16),
-        pltpu.VMEM((ring, tok_rows, feat), BF16),
-        pltpu.VMEM((ring, tok_rows, feat), BF16),
+        pltpu.VMEM((2 * chain, tok_rows, feat), BF16),
+        pltpu.VMEM((2 * chain, tok_rows, feat), BF16),
         pltpu.VMEM((ring, 8, experts), F32),
         pltpu.VMEM((CHUNKS, n_exp * rows, per_chunk * tok_rows), BF16),
         pltpu.VMEM((CHUNKS, n_exp * rows, 128), F32),
         pltpu.VMEM((CHUNKS, n_exp, 2, rows, feat), BF16),
         pltpu.VMEM((CHUNKS, plane, 2, rows, feat), BF16),
-        pltpu.VMEM((CHUNKS, n_tp, 3, part, half), BF16),
-        pltpu.VMEM((CHUNKS, n_tp - 1, 3, part, half), BF16),
-        pltpu.VMEM((CHUNKS, n_tp, 3, part, half), BF16),
+        pltpu.VMEM((CHUNKS, n_tp, 3, strip, half), BF16),
+        pltpu.VMEM((CHUNKS, n_tp - 1, 3, strip, half), BF16),
+        pltpu.VMEM((CHUNKS, n_tp, 3, strip, half), BF16),
         pltpu.VMEM((feat, half), F32),
         pltpu.VMEM((feat, half), F32),
         pltpu.VMEM((half, feat), F32),
@@ -500,22 +571,25 @@
         pltpu.VMEM((feat, half), BF16),
         pltpu.VMEM((half, feat), BF16),
         pltpu.SemaphoreType.DMA((8,)),
+        pltpu.SemaphoreType.DMA((3,)),
+        pltpu.SemaphoreType.DMA((2, chain, len(legs))),
+        pltpu.SemaphoreType.DMA((CHUNKS,)),
+        pltpu.SemaphoreType.DMA((CHUNKS, plane - 1)),
+        pltpu.SemaphoreType.DMA((CHUNKS,)),
+        pltpu.SemaphoreType.DMA((CHUNKS, n_tp - 1)),
+        pltpu.SemaphoreType.DMA((CHUNKS,)),
+        pltpu.SemaphoreType.DMA((CHUNKS, n_tp - 1)),
+        pltpu.SemaphoreType.DMA((CHUNKS,)),
+        pltpu.SemaphoreType.DMA((CHUNKS, plane - 1)),
+        pltpu.SemaphoreType.DMA((2,)),
+        pltpu.SemaphoreType.DMA((2, chain, 2, PARTS)),
+        pltpu.SemaphoreType.DMA((2 * CHUNKS,)),
+        pltpu.VMEM((n_exp * rows, 2 * quarter * SHARED), BF16),
+        pltpu.VMEM((2, 2, chain, SHARED, feat), BF16),
+        pltpu.VMEM((2, CHUNKS, 2 * quarter, SHARED, feat), BF16),
+        pltpu.SemaphoreType.DMA((3,)),
         pltpu.SemaphoreType.DMA((2, chain, 3)),
-        pltpu.SemaphoreType.DMA((2, chain, 3)),
-        pltpu.SemaphoreType.DMA((CHUNKS, plane - 1)),
-        pltpu.SemaphoreType.DMA((CHUNKS, plane - 1)),
-        pltpu.SemaphoreType.DMA((CHUNKS, n_tp - 1)),
-        pltpu.SemaphoreType.DMA((CHUNKS, n_tp - 1)),
-        pltpu.SemaphoreType.DMA((CHUNKS, n_tp - 1)),
-        pltpu.SemaphoreType.DMA((CHUNKS, n_tp - 1)),
-        pltpu.SemaphoreType.DMA((CHUNKS, plane - 1)),
-        pltpu.SemaphoreType.DMA((CHUNKS, plane - 1)),
-        pltpu.SemaphoreType.DMA((2, chain, 2)),
-        pltpu.SemaphoreType.DMA((2, chain, 2)),
-        pltpu.SemaphoreType.DMA((2 * CHUNKS,)),
-        pltpu.SemaphoreType.DMA((2, chain, 3)),
-        pltpu.SemaphoreType.DMA((2, chain, 3)),
-        pltpu.SemaphoreType.DMA((2, chain, 2)),
+        pltpu.SemaphoreType.DMA((2,)),
         pltpu.SemaphoreType.DMA((2, chain, 2)),
     ]
     return kernel, scratch

time: 154 us -> 134 us (0.87)
  Pallas kernels: 153 us -> 133 us
    pallas_call x1, Pallas kernels: 151 us -> 131 us  [shards(): pl.pallas_call(kernel, out_shape=(jax.ShapeDtypeStruct((tok_rows, feat),...]
where the time goes in v3:
time: 134 us
  Pallas kernels  133 us (99%)
    pallas_call x1, Pallas kernels, shards(): pl.pallas_call(kernel, out_shape=(jax.ShapeDtypeStruct((tok_rows, feat),...  131 us

profile of v3, /device:TPU:32, one launch (start us, length us, event | category | flops | bytes accessed | tf_op | source)
XLA Modules:
  0.0 133.7 jit_solution(7290351312110949357)
XLA Ops:
  0.6 130.9 %routed_experts.1 = (bf16[32,512]{1,0:T(8,128)(2,1)}, bf16[32,512]{1,0:T(8,128)(2,1)}, bf16[1,512,384]{2,1,0:T(8,128)(2,1)}, bf16[1,512,384]{2,1,0:T(8,128)(2,1)}, bf16[1,384,512]{2,1,0:T(8,128)(2,1)}) custom-call(bf16[32,512]{1,0:T(8,128)(2,1)} %tok_ref.1, bf16[32,512]{1,0:T(8,128)(2,1)} %grd_ref.1, s32[8,32]{1,0:T(8,128)} %bitcast.2, f32[8,32]{1,0:T(8,128)} %bitcast.3, ...), custom_call_target="tpu_custom_call" | custom-call | tf_op jit(solution)/shard_map/routed_experts/pallas_call | solution.py:634
  131.6 2.1 %deliver.1 = (bf16[32,512]{1,0:T(8,128)(2,1)}, bf16[32,512]{1,0:T(8,128)(2,1)}, bf16[1,512,384]{2,1,0:T(8,128)(2,1)}, bf16[1,512,384]{2,1,0:T(8,128)(2,1)}, bf16[1,384,512]{2,1,0:T(8,128)(2,1)}) custom-call(bf16[32,512]{1,0:T(8,128)(2,1)} %get-tuple-element.10.refs_0_, bf16[32,512]{1,0:T(8,128)(2,1)} %get-tuple-element.11.refs_1_, ...), custom_call_target="tpu_custom_call" | custom-call | tf_op jit(solution)/shard_map/deliver/pallas_call | solution.py:615
